TPU v7x, 32 devices: a whole 2x2x4 slice. The times are simulated.
32 devices in a mesh: vx: 2 (over x), vy: 4 (over y, core), scan: 4 (over z).
Axes of the slice: x: 2, y: 2, z: 4, core: 2. Of those that a mesh axis runs over, the one named last changes fastest.
Arguments:
- volume: bfloat16 [2, 64, 256, 256], P(None, 'vx', 'vy'), may hold values from -6 to 6
- tile_matrix: bfloat16 [4, 2, 8, 1024, 128], P('scan', 'vx', 'vy'), may hold values from -0.09375 to 0.09375
- tile_offset: int32 [4, 2, 8], P('scan', 'vx', 'vy'), may hold values from 0 to 384
- patch_count: int32 [4, 8], P('scan', ('vx', 'vy')), may hold values from 1 to 3, as said below
- scan_position: int32 [4, 8, 3, 2], P('scan', ('vx', 'vy')), may hold values from 0 to 256, as said below
- measured: float32 [4, 8, 3, 256, 256], P('scan', ('vx', 'vy')), may hold values from 0.2 to 5
- illumination: float32 [2, 256, 256], replicated, may hold values from -6 to 6
Outputs:
- change: float32 [2, 64, 256, 256], P(None, 'vx', 'vy', 'scan')
Inputs may be any that keep to these rules, and one draw needn't show every extreme that they name: `patch_count`: an owner's slots below its count hold measured patches, the others are unused; at every angle some owner holds 3. `scan_position`: column 0 is a patch's first detector column, 0 to 256; column 1 its first row, 0 to 0.
All inputs are finite; a program needn't handle non-finite values.
Results may differ from a plain program's by a relative error of at most 0.0085.
Values may be sent and summed in bfloat16 or wider, within the bound.
No kernel may reach another device: no remote copies, remote signals or barrier semaphores. Data moves between devices by JAX's collectives and lax.ppermute only.
A program may use at most 64 MiB of HBM per device.

v0:
```python
import math
import jax
import jax.numpy as jnp
from jax import lax
from jax.sharding import PartitionSpec as P

TILE = 32
NZ = 256
U = 512
TU = 128
PATCH_SIDE = 256
ABSORPTION = 0.2
STEP_LENGTH = 0.003


def dft_tables(length):
    counter = jnp.arange(length, dtype=jnp.int32)
    product = counter[:, None] * counter[None, :] % length
    radians = product.astype(jnp.float32) * (2.0 * math.pi / length)
    scaling = 1.0 / math.sqrt(length)
    return (jnp.cos(radians) * scaling, jnp.sin(radians) * scaling)


def matmul(left, right):
    return jnp.dot(left, right, precision=lax.Precision.HIGHEST)


def patch_misfit(window, illumination, intensity, cosine_table, sine_table):
    amplitude = jnp.exp(-ABSORPTION * window[1])
    trans_re = amplitude * jnp.cos(window[0])
    trans_im = amplitude * jnp.sin(window[0])
    exit_re = illumination[0] * trans_re - illumination[1] * trans_im
    exit_im = illumination[0] * trans_im + illumination[1] * trans_re
    half_re = matmul(cosine_table, exit_re) + matmul(sine_table, exit_im)
    half_im = matmul(cosine_table, exit_im) - matmul(sine_table, exit_re)
    far_re = matmul(half_re, cosine_table) + matmul(half_im, sine_table)
    far_im = matmul(half_im, cosine_table) - matmul(half_re, sine_table)
    residue = far_re * far_re + far_im * far_im - intensity
    return jnp.sum(residue * residue)


def place_patch(summed_total, slope, corner):
    anchor = (jnp.zeros((), jnp.int32), corner[0], corner[1])
    before = lax.dynamic_slice(summed_total, anchor, slope.shape)
    return lax.dynamic_update_slice(summed_total, before + slope, anchor)


def patch_term(
    summed_total, projected_field, corner, intensity, illumination, cosine_table, sine_table
):
    anchor = (jnp.zeros((), jnp.int32), corner[0], corner[1])
    window = lax.dynamic_slice(projected_field, anchor, (2, PATCH_SIDE, PATCH_SIDE))
    slope = jax.grad(patch_misfit)(window, illumination, intensity, cosine_table, sine_table)
    return place_patch(summed_total, slope, corner)


def brick_tiles(field):
    components, width_x, width_y, depth_cells = field.shape
    blocks = field.reshape(components, width_x // TILE, TILE, width_y // TILE, TILE, depth_cells)
    blocks = blocks.transpose(1, 3, 0, 2, 4, 5)
    return blocks.reshape(-1, components, TILE * TILE, depth_cells)


def tiles_brick(blocks, width_x, width_y):
    components = blocks.shape[1]
    depth_cells = blocks.shape[3]
    shaped = blocks.reshape(width_x // TILE, width_y // TILE, components, TILE, TILE, depth_cells)
    return shaped.transpose(2, 0, 3, 1, 4, 5).reshape(components, width_x, width_y, depth_cells)


def partial_projection(current, matrices, offsets):
    blocks = brick_tiles(current)
    tile_parts = jnp.einsum("tku,tckz->tcuz", matrices, blocks, preferred_element_type=jnp.float32)
    summed_total = jnp.zeros((2, U, NZ), jnp.float32)
    for tile_index in range(tile_parts.shape[0]):
        anchor = (jnp.zeros((), jnp.int32), offsets[tile_index], jnp.zeros((), jnp.int32))
        before = lax.dynamic_slice(summed_total, anchor, tile_parts.shape[1:])
        summed_total = lax.dynamic_update_slice(
            summed_total, before + tile_parts[tile_index], anchor
        )
    return summed_total


def cut_windows(image, offsets):

    def cut_window(offset):
        anchor = (jnp.zeros((), jnp.int32), offset, jnp.zeros((), jnp.int32))
        return lax.dynamic_slice(image, anchor, (2, TU, NZ))

    return jax.vmap(cut_window)(offsets)


def back_tiles(matrices, windows, width_x, width_y):
    blocks = jnp.einsum("tku,tcuz->tckz", matrices, windows, preferred_element_type=jnp.float32)
    return tiles_brick(blocks, width_x, width_y)


def per_device(
    volume, tile_matrix, tile_offset, patch_count, scan_position, measured, illumination
):
    cosine_table, sine_table = dft_tables(PATCH_SIDE)
    matrices = tile_matrix[0].reshape(-1, TILE * TILE, TU)
    offsets = tile_offset[0].reshape(-1)
    live_count = patch_count[0, 0]
    positions = scan_position[0, 0]
    intensity_values = measured[0, 0]
    width_x = volume.shape[1]
    width_y = volume.shape[2]
    slab_depth = NZ // lax.axis_size("scan")
    slab_start = lax.axis_index("scan") * slab_depth

    def own_slot(slot_index, running, projected_field):
        return patch_term(
            running,
            projected_field,
            positions[slot_index],
            intensity_values[slot_index],
            illumination,
            cosine_table,
            sine_table,
        )

    iterate = lax.dynamic_slice_in_dim(volume, slab_start, slab_depth, 3).astype(jnp.float32)
    projected_field = lax.psum(partial_projection(volume, matrices, offsets), ("vx", "vy"))
    image = lax.psum(
        lax.fori_loop(
            0,
            live_count,
            lambda slot_index, running: own_slot(slot_index, running, projected_field),
            jnp.zeros_like(projected_field),
        ),
        ("vx", "vy"),
    )
    windows = cut_windows(image, offsets).astype(jnp.bfloat16)
    slope = back_tiles(matrices, windows, width_x, width_y)
    slope_sum = lax.psum_scatter(
        slope.astype(jnp.bfloat16), "scan", scatter_dimension=3, tiled=True
    ).astype(jnp.float32)
    iterate = iterate - STEP_LENGTH * slope_sum
    return iterate - lax.dynamic_slice_in_dim(volume, slab_start, slab_depth, 3).astype(jnp.float32)


def solution(mesh):
    in_specs = (
        P(None, "vx", "vy", None),
        P("scan", "vx", "vy", None, None),
        P("scan", "vx", "vy"),
        P("scan", ("vx", "vy")),
        P("scan", ("vx", "vy"), None, None),
        P("scan", ("vx", "vy"), None, None, None),
        P(),
    )
    out_specs = P(None, "vx", "vy", "scan")
    return jax.shard_map(
        per_device, mesh=mesh, in_specs=in_specs, out_specs=out_specs, check_vma=False
    )
```

profile of v0, /device:TPU:0, one launch (start us, length us, event | category | flops | bytes accessed | tf_op | source)
XLA Modules:
  0.0 327.8 jit_solution(10603027786342075903)
XLA Ops:
  6.5 0.0 copy-start
  6.5 0.0 all-reduce.6.cloned.1.call-start
  6.5 1.3 fusion.124
  10.4 1.8 copy.25
  12.2 0.0 copy-done
  12.2 1.0 convolution_bitcast_fusion
  13.2 0.0 copy-start.5
  14.5 0.1 broadcast.46
  14.7 0.0 copy-start.7
  14.7 1.6 dynamic_update_slice.10
  16.3 0.0 copy-start.6
  16.3 0.1 fusion.117
  16.5 1.6 dynamic_update_slice.11
  18.1 0.0 copy-start.3
  18.1 1.0 copy-done.3
  19.1 0.0 all-reduce.6.cloned.1.call-update
  19.1 0.0 reduce-scatter.4.cloned.1.call-start
  19.2 0.0 copy-done.5
  19.2 0.2 copy.27
  19.4 0.0 copy-done.7
  19.4 59.3 %all-reduce.6.cloned.1.call-done = f32[2,512,256]{1,2,0:T(8,128)} async-done(((f32[2,512,256]{1,2,0:T(8,128)}), f32[2,512,256]{1,2,0:T(8,128)}) %all-reduce.6.cloned.1.call-update) | async-done | bytes 1048592 | tf_op jit(solution)/shard_map/psum | solution.py:124
  78.7 1.2 broadcast.46.clone
  79.9 0.0 copy-done.6
  79.9 51.8 %while.12 = (s32[]{:T(128)}, f32[2,512,256]{2,0,1:T(2,128)}, s32[]{:T(128)}, s32[3,2]{0,1:T(2,128)S(1)}, f32[2,512,256]{1,2,0:T(8,128)}, /*index=5*/f32[2,256,25...) while((s32[]{:T(128)}, f32[2,512,256]{2,0,1:T(2,128)}, ...), condition=%wide.region_2.3_spmd.clone.clone, body=%wide.region_1.2_spmd.clone.clone.sunk | while | flops 3240427520 | bytes 30671164 | solution.py:126
  98.5 0.1 constant_dynamic-slice_fusion.4
  98.6 0.5 slice.79
  101.0 2.2 fusion.184
  103.2 1.4 fusion.185
  104.6 1.4 convolution_subtract_fusion.4
  106.0 1.5 fusion.186
  107.4 1.4 fusion.187
  108.8 1.4 convolution_add_fusion.9
  110.2 1.5 convolution_subtract_fusion.5
  111.7 1.5 fusion.188
  113.1 2.4 add_multiply_fusion.3
  115.6 1.4 fusion.191
  117.0 1.4 convolution_add_fusion.11
  118.3 1.4 fusion.189
  119.7 1.4 convolution_add_fusion.10
  121.1 1.5 fusion.190
  122.6 1.5 fusion.192
  124.1 1.5 fusion.193
  125.5 0.0 copy-start.2
  125.5 2.4 fusion.194
  128.0 1.2 fusion.195
  129.2 0.0 copy-done.2
  129.2 0.2 constant_dynamic-slice_fusion.5
  129.4 0.2 copy.43
  129.6 0.1 add_add_fusion.2
  129.7 0.2 copy.44
  129.9 1.0 constant_dynamic-update-slice_fusion.2
  131.7 112.3 %all-reduce.7 = bf16[2,512,256]{2,0,1:T(2,128)(2,1)S(1)} all-reduce(f32[2,512,256]{2,0,1:T(2,128)} %get-tuple-element.94), channel_id=1, replica_groups=mesh['vx'=2,'vy'=4,'scan'=4] {'vx','vy'}, use_global_device_ids=true, to_apply=%region_3.4 | all-reduce | flops 262144 | bytes 1572864 | tf_op jit(solution)/shard_map/psum | solution.py:125
  244.1 1.1 gather_fusion
  245.1 0.8 convert_bitcast_fusion
  245.9 2.6 copy.30
  248.5 1.8 copy.31
  250.3 6.7 %copy.34 = bf16[2,32,64,256]{2,1,0,3:T(8,128)(2,1)} copy(bf16[2,32,64,256]{3,2,1,0:T(8,128)(2,1)S(1)} %bitcast.209) | data formatting | bytes 4194304
  257.0 6.6 %reshape.60 = bf16[256,4096]{1,0:T(8,128)(2,1)} reshape(bf16[256,2,32,64]{3,2,1,0:T(8,128)(2,1)} %bitcast.208) | data formatting | bytes 4194304
  263.6 0.0 reduce-scatter.4.cloned.1.call-update
  263.6 0.0 copy-start.4
  263.6 48.2 %reduce-scatter.4.cloned.1.call-done = bf16[64,4096]{1,0:T(8,128)(2,1)} async-done(((bf16[256,4096]{1,0:T(8,128)(2,1)}), bf16[64,4096]{1,0:T(8,128)(2,1)}) %reduce-scatter.4.cloned.1.call-update) | async-done | bytes 524304
  311.8 2.7 reshape.61
  314.6 2.9 copy.35
  317.5 3.1 subtract_subtract_fusion
  (5 shorter events, 0.0 us)
Async XLA Ops:
  6.5 5.7 %copy-start = (bf16[1,1,2,1024,128]{4,3,2,1,0:T(8,128)(2,1)S(1)}, bf16[1,1,2,1024,128]{4,3,2,1,0:T(8,128)(2,1)}, u32[]{:S(2)}) copy-start(bf16[1,1,2,1024,128]{4,3,2,1,0:T(8,128)(2,1)} %param.10) | copy-start | bytes 1572868
  6.5 72.2 %all-reduce.6.cloned.1.call-start = ((), (), s32[]{:S(2)}) async-start(), calls=%async_computation.1 | async-start | bytes 2097152 | tf_op jit(solution)/shard_map/psum | solution.py:124
  13.2 6.0 %copy-start.5 = (f32[2,256,256]{2,1,0:T(8,128)S(1)}, f32[2,256,256]{2,1,0:T(8,128)}, u32[]{:S(2)}) copy-start(f32[2,256,256]{2,1,0:T(8,128)} %param.15) | copy-start | bytes 1572868
  14.7 4.7 %copy-start.7 = (s32[1,1,2]{2,1,0:T(1,128)S(1)}, s32[1,1,2]{2,1,0:T(1,128)}, u32[]{:S(2)}) copy-start(s32[1,1,2]{2,1,0:T(1,128)} %param.11) | copy-start | bytes 28
  16.3 63.6 %copy-start.6 = (s32[1,1,3,2]{2,3,1,0:T(2,128)S(1)}, s32[1,1,3,2]{2,3,1,0:T(2,128)}, u32[]{:S(2)}) copy-start(s32[1,1,3,2]{2,3,1,0:T(2,128)} %param.13) | copy-start | bytes 76
  18.1 1.0 copy-start.3
  19.1 292.7 %reduce-scatter.4.cloned.1.call-start = ((), (), s32[]{:S(2)}) async-start(), calls=%async_computation.2 | async-start | bytes 2621440
  121.1 4.4 %copy-start.1 = (f32[2,512,256]{1,2,0:T(8,128)S(1)}, f32[2,512,256]{1,2,0:T(8,128)}, u32[]{:S(2)}) copy-start(f32[2,512,256]{1,2,0:T(8,128)} %get-tuple-element.294) | copy-start | bytes 3145732 | tf_op jit(solution)/shard_map/while
  125.5 3.6 %copy-start.2 = (f32[2,512,256]{2,0,1:T(2,128)S(1)}, f32[2,512,256]{2,0,1:T(2,128)}, u32[]{:S(2)}) copy-start(f32[2,512,256]{2,0,1:T(2,128)} %get-tuple-element.279) | copy-start | bytes 3145732 | tf_op jit(solution)/shard_map/while
  263.6 53.9 %copy-start.4 = (bf16[2,32,64,256]{3,2,1,0:T(8,128)(2,1)S(1)}, bf16[2,32,64,256]{3,2,1,0:T(8,128)(2,1)}, u32[]{:S(2)}) copy-start(bf16[2,32,64,256]{3,2,1,0:T(8,128)(2,1)} %param.9) | copy-start | bytes 6291460
Sparse Core Ops, SparseCore 0:
  19.2 59.4 all-reduce.5
  263.7 48.0 reduce-scatter.3
where the time goes:
time: 331 us; the launch traced here: 328 us
  blocking collectives  112 us (34%)
  waiting for transfers between devices  107 us (32%)
  local copies, waits for them, and re-layouts  35.6 us (11%)
  matrix products  26.3 us (8%)
  loops' own time  21.5 us (6%)
  between operations  17.9 us (5%)
  other arithmetic  6.69 us (2%)
    psum x1, blocking collectives, per_device(): lax.psum(lax.fori_loop(0, live_count, lambda slot_index, running: own_slo...  112 us
    psum x1, waiting for transfers between devices, per_device(): lax.psum(partial_projection(volume, matrices, offsets), ('vx', 'vy'))  59.3 us
    unnamed x3, waiting for transfers between devices  48.2 us
    dot_general x16, matrix products, matmul(): return jnp.dot(left, right, precision=lax.Precision.HIGHEST)  24.6 us
    another operation x1, loops' own time, per_device(): lax.fori_loop(0, live_count, lambda slot_index, running: own_slot(slot_in...  21.5 us
    unnamed x17, local copies, waits for them, and re-layouts  20.1 us
  transfers between devices with their start and end apart: 2, of which 2 were waited for; matrix products, arithmetic and copies ran while one was open for 0% of the time, Pallas kernels for 0%

commit v1 on v0

--- a/solution.py
+++ b/solution.py
@@ -123,13 +123,16 @@
     iterate = lax.dynamic_slice_in_dim(volume, slab_start, slab_depth, 3).astype(jnp.float32)
     projected_field = lax.psum(partial_projection(volume, matrices, offsets), ("vx", "vy"))
     image = lax.psum(
-        lax.fori_loop(
-            0,
-            live_count,
-            lambda slot_index, running: own_slot(slot_index, running, projected_field),
-            jnp.zeros_like(projected_field),
+        lax.psum(
+            lax.fori_loop(
+                0,
+                live_count,
+                lambda slot_index, running: own_slot(slot_index, running, projected_field),
+                jnp.zeros_like(projected_field),
+            ),
+            "vy",
         ),
-        ("vx", "vy"),
+        "vx",
     )
     windows = cut_windows(image, offsets).astype(jnp.bfloat16)
     slope = back_tiles(matrices, windows, width_x, width_y)

time: 331 us -> 345 us (1.042)
  waiting for transfers between devices: 107 us -> 205 us
  blocking collectives: 112 us -> 28.5 us
    psum x0 -> x1, waiting for transfers between devices: none -> 102 us  [per_device(): lax.psum(lax.fori_loop(0, live_count, lambda slot_index, running: own_slo...]
    psum x1, blocking collectives: 112 us -> 28.5 us  [per_device(): lax.psum(lax.psum(lax.fori_loop(0, live_count, lambda slot_index, running...]
    unnamed x3 -> x4, waiting for transfers between devices: 48.2 us -> 44.1 us
  transfers between devices with their start and end apart: 2 -> 3, of which waited for: 2 -> 3; matrix products, arithmetic and copies ran while one was open for 0% -> 0% of each run, Pallas kernels for 0% -> 0%
where the time goes in v1:
time: 345 us; the launch traced here: 341 us
  waiting for transfers between devices  205 us (59%)
  local copies, waits for them, and re-layouts  35.6 us (10%)
  blocking collectives  28.5 us (8%)
  matrix products  26.3 us (8%)
  loops' own time  21.5 us (6%)
  between operations  17.6 us (5%)
  other arithmetic  6.69 us (2%)
    psum x1, waiting for transfers between devices, per_device(): lax.psum(lax.fori_loop(0, live_count, lambda slot_index, running: own_slo...  102 us
    psum x1, waiting for transfers between devices, per_device(): lax.psum(partial_projection(volume, matrices, offsets), ('vx', 'vy'))  59.3 us
    unnamed x4, waiting for transfers between devices  44.1 us
    psum x1, blocking collectives, per_device(): lax.psum(lax.psum(lax.fori_loop(0, live_count, lambda slot_index, running...  28.5 us
    dot_general x16, matrix products, matmul(): return jnp.dot(left, right, precision=lax.Precision.HIGHEST)  24.6 us
    another operation x1, loops' own time, per_device(): lax.fori_loop(0, live_count, lambda slot_index, running: own_slot(slot_in...  21.5 us
    unnamed x17, local copies, waits for them, and re-layouts  20.1 us
  transfers between devices with their start and end apart: 3, of which 3 were waited for; matrix products, arithmetic and copies ran while one was open for 0% of the time, Pallas kernels for 0%

profile of v1, /device:TPU:0, one launch (start us, length us, event | category | flops | bytes accessed | tf_op | source)
XLA Modules:
  0.0 341.2 jit_solution(16040897933049914428)
XLA Ops:
  6.5 0.0 copy-start
  6.5 0.0 all-reduce.7.cloned.1.call-start
  6.5 1.3 fusion.124
  10.4 1.8 copy.25
  12.2 0.0 copy-done
  12.2 1.0 convolution_bitcast_fusion
  13.2 0.0 copy-start.5
  14.5 0.1 broadcast.46
  14.7 1.6 dynamic_update_slice.10
  16.3 0.0 copy-start.6
  16.3 0.1 fusion.117
  16.5 1.6 dynamic_update_slice.11
  18.1 0.0 copy-start.3
  18.1 1.0 copy-done.3
  19.1 0.0 all-reduce.7.cloned.1.call-update
  19.1 0.0 all-reduce.9.cloned.1.call-start
  19.2 0.0 copy-done.5
  19.2 0.2 copy.27
  19.4 59.3 %all-reduce.7.cloned.1.call-done = f32[2,512,256]{1,2,0:T(8,128)} async-done(((f32[2,512,256]{1,2,0:T(8,128)}), f32[2,512,256]{1,2,0:T(8,128)}) %all-reduce.7.cloned.1.call-update) | async-done | bytes 1048592 | tf_op jit(solution)/shard_map/psum | solution.py:124
  78.7 1.2 broadcast.46.clone
  79.9 0.0 copy-done.6
  79.9 51.8 %while.12 = (s32[]{:T(128)}, f32[2,512,256]{2,0,1:T(2,128)}, s32[]{:T(128)}, s32[3,2]{0,1:T(2,128)S(1)}, f32[2,512,256]{1,2,0:T(8,128)}, /*index=5*/f32[2,256,25...) while((s32[]{:T(128)}, f32[2,512,256]{2,0,1:T(2,128)}, ...), condition=%wide.region_2.3_spmd.clone.clone, body=%wide.region_1.2_spmd.clone.clone.sunk | while | flops 3240427520 | bytes 30671164 | solution.py:127
  98.5 0.1 constant_dynamic-slice_fusion.4
  98.6 0.5 slice.79
  101.0 2.2 fusion.184
  103.2 1.4 fusion.185
  104.6 1.4 convolution_subtract_fusion.4
  106.0 1.5 fusion.186
  107.5 1.4 fusion.187
  108.8 1.4 convolution_add_fusion.9
  110.2 1.5 convolution_subtract_fusion.5
  111.7 1.5 fusion.188
  113.1 2.4 add_multiply_fusion.3
  115.6 1.4 fusion.191
  117.0 1.4 convolution_add_fusion.11
  118.3 1.4 fusion.189
  119.7 1.4 convolution_add_fusion.10
  121.1 1.5 fusion.190
  122.6 1.5 fusion.192
  124.1 1.5 fusion.193
  125.5 0.0 copy-start.2
  125.6 2.4 fusion.194
  128.0 1.2 fusion.195
  129.2 0.2 constant_dynamic-slice_fusion.5
  129.4 0.2 copy.43
  129.6 0.1 add_add_fusion.2
  129.7 0.2 copy.44
  129.9 1.0 constant_dynamic-update-slice_fusion.2
  131.8 0.0 all-reduce.9.cloned.1.call-update
  131.8 0.0 reduce-scatter.4.cloned.1.call-start
  131.8 101.6 %all-reduce.9.cloned.1.call-done = f32[2,512,256]{2,0,1:T(2,128)} async-done(((f32[2,512,256]{2,0,1:T(2,128)}), f32[2,512,256]{2,0,1:T(2,128)}) %all-reduce.9.cloned.1.call-update) | async-done | bytes 1048592 | tf_op jit(solution)/shard_map/psum | solution.py:126
  233.4 28.5 %all-reduce.10 = bf16[2,512,256]{2,0,1:T(2,128)(2,1)S(1)} all-reduce(f32[2,512,256]{2,0,1:T(2,128)} %all-reduce.9.cloned.1.call-done), channel_id=1, replica_groups=mesh['vx'=2,'vy'=4,'scan'=4] {'vx'}, use_global_device_ids=true, to_apply=%region_4.5 | all-reduce | flops 262144 | bytes 1572864 | tf_op jit(solution)/shard_map/psum | solution.py:125
  261.9 1.1 gather_fusion
  263.0 0.8 convert_bitcast_fusion
  263.8 2.6 copy.30
  266.3 1.8 copy.31
  268.2 6.7 %copy.34 = bf16[2,32,64,256]{2,1,0,3:T(8,128)(2,1)} copy(bf16[2,32,64,256]{3,2,1,0:T(8,128)(2,1)S(1)} %bitcast.209) | data formatting | bytes 4194304
  274.9 6.6 %reshape.60 = bf16[256,4096]{1,0:T(8,128)(2,1)} reshape(bf16[256,2,32,64]{3,2,1,0:T(8,128)(2,1)} %bitcast.208) | data formatting | bytes 4194304
  281.5 0.0 reduce-scatter.4.cloned.1.call-update
  281.5 0.0 copy-start.4
  281.5 44.1 %reduce-scatter.4.cloned.1.call-done = bf16[64,4096]{1,0:T(8,128)(2,1)} async-done(((bf16[256,4096]{1,0:T(8,128)(2,1)}), bf16[64,4096]{1,0:T(8,128)(2,1)}) %reduce-scatter.4.cloned.1.call-update) | async-done | bytes 524304
  325.6 2.7 reshape.61
  328.3 2.9 copy.35
  331.3 3.1 subtract_subtract_fusion
  (8 shorter events, 0.0 us)
Async XLA Ops:
  6.5 5.7 %copy-start = (bf16[1,1,2,1024,128]{4,3,2,1,0:T(8,128)(2,1)S(1)}, bf16[1,1,2,1024,128]{4,3,2,1,0:T(8,128)(2,1)}, u32[]{:S(2)}) copy-start(bf16[1,1,2,1024,128]{4,3,2,1,0:T(8,128)(2,1)} %param.10) | copy-start | bytes 1572868
  6.5 72.1 %all-reduce.7.cloned.1.call-start = ((), (), s32[]{:S(2)}) async-start(), calls=%async_computation.1 | async-start | bytes 2097152 | tf_op jit(solution)/shard_map/psum | solution.py:124
  13.2 6.0 %copy-start.5 = (f32[2,256,256]{2,1,0:T(8,128)S(1)}, f32[2,256,256]{2,1,0:T(8,128)}, u32[]{:S(2)}) copy-start(f32[2,256,256]{2,1,0:T(8,128)} %param.15) | copy-start | bytes 1572868
  16.3 63.6 %copy-start.6 = (s32[1,1,3,2]{2,3,1,0:T(2,128)S(1)}, s32[1,1,3,2]{2,3,1,0:T(2,128)}, u32[]{:S(2)}) copy-start(s32[1,1,3,2]{2,3,1,0:T(2,128)} %param.13) | copy-start | bytes 76
  18.1 1.0 copy-start.3
  19.1 214.3 %all-reduce.9.cloned.1.call-start = ((), (), s32[]{:S(2)}) async-start(), calls=%async_computation.2 | async-start | bytes 2097152 | tf_op jit(solution)/shard_map/psum | solution.py:126
  79.9 51.9 %copy-start.7 = (s32[1,1,2]{2,1,0:T(1,128)S(1)}, s32[1,1,2]{2,1,0:T(1,128)}, u32[]{:S(2)}) copy-start(s32[1,1,2]{2,1,0:T(1,128)} %param.11) | copy-start | bytes 28
  121.1 4.4 %copy-start.1 = (f32[2,512,256]{1,2,0:T(8,128)S(1)}, f32[2,512,256]{1,2,0:T(8,128)}, u32[]{:S(2)}) copy-start(f32[2,512,256]{1,2,0:T(8,128)} %get-tuple-element.294) | copy-start | bytes 3145732 | tf_op jit(solution)/shard_map/while
  125.5 3.6 %copy-start.2 = (f32[2,512,256]{2,0,1:T(2,128)S(1)}, f32[2,512,256]{2,0,1:T(2,128)}, u32[]{:S(2)}) copy-start(f32[2,512,256]{2,0,1:T(2,128)} %get-tuple-element.279) | copy-start | bytes 3145732 | tf_op jit(solution)/shard_map/while
  131.8 193.8 %reduce-scatter.4.cloned.1.call-start = ((), (), s32[]{:S(2)}) async-start(), calls=%async_computation.3 | async-start | bytes 2621440
  281.5 49.8 %copy-start.4 = (bf16[2,32,64,256]{3,2,1,0:T(8,128)(2,1)S(1)}, bf16[2,32,64,256]{3,2,1,0:T(8,128)(2,1)}, u32[]{:S(2)}) copy-start(bf16[2,32,64,256]{3,2,1,0:T(8,128)(2,1)} %param.9) | copy-start | bytes 6291460
Sparse Core Ops, SparseCore 0:
  19.2 59.4 all-reduce.6
  131.9 101.5 all-reduce.8
  281.6 43.9 reduce-scatter.3
